TPU v7x, 128 devices: a whole 4x4x4 slice. The times are simulated.
128 devices in a mesh: req: 32 (over y, z, core), tp: 4 (over x).
Axes of the slice: x: 4, y: 4, z: 4, core: 2. Of those that a mesh axis runs over, the one named last changes fastest.
Arguments:
- states: bfloat16 [64, 512, 1024], P('req', 'tp'), may hold values from -45 to 45
- lengths: int32 [64], P('req'), may hold values from 3 to 512, as said below
- w_qkv: bfloat16 [1024, 3, 1024], P(None, None, 'tp'), may hold values from -0.1875 to 0.1875
- b_qkv: float32 [3, 1024], P(None, 'tp'), may hold values from -3 to 3
- w_out: bfloat16 [1024, 1024], P('tp'), may hold values from -0.1875 to 0.1875
- b_out: float32 [1024], replicated, may hold values from -3 to 3
- ln1_gain: float32 [1024], replicated, may hold values from 0.1 to 1.9
- ln1_shift: float32 [1024], replicated, may hold values from -3 to 3
- w_up: bfloat16 [1024, 4096], P(None, 'tp'), may hold values from -0.1875 to 0.1875
- b_up: float32 [4096], P('tp'), may hold values from -3 to 3
- w_down: bfloat16 [4096, 1024], P('tp'), may hold values from -0.09375 to 0.09375
- b_down: float32 [1024], replicated, may hold values from -3 to 3
- ln2_gain: float32 [1024], replicated, may hold values from 0.1 to 1.9
- ln2_shift: float32 [1024], replicated, may hold values from -3 to 3
- index_rows: bfloat16 [524288, 1024], P(('req', 'tp')), may hold values from -0.1875 to 0.1875
- cand_ids: int32 [64, 64], P('req', 'tp'), may hold values from 0 to 524287
Outputs:
- hidden_out: bfloat16 [64, 512, 1024], P('req', 'tp')
- scores: float32 [64, 64], P('req', 'tp')
Inputs may be any that keep to these rules, and one draw needn't show every extreme that they name: Valid positions are the first lengths ones of a text; in every draw some text has 512.
All inputs are finite; a program needn't handle non-finite values.
Results may differ from a plain program's by a relative error of at most 0.015.
Values may be sent and summed in bfloat16 or wider, within the bound.
A program may use at most 128 MiB of HBM per device.

v0:
```python
import jax
import jax.numpy as jnp
from jax import lax
from jax.sharding import PartitionSpec as P

HEAD_DIM = 64
WINDOW = 512
layer_eps = 1e-05
norm_eps = 1e-06


def layer_norm(values, gain, shift):
    centre = values - jnp.mean(values, axis=-1, keepdims=True)
    spread = jnp.mean(centre * centre, axis=-1, keepdims=True)
    return centre * lax.rsqrt(spread + layer_eps) * gain + shift


def window_attention(queries_h, keys_h, values_h, lengths):
    seq_len = queries_h.shape[1]
    half_window = WINDOW // 2
    scale_factor = HEAD_DIM ** (-0.5)
    pos = jnp.arange(seq_len, dtype=jnp.int32)
    near = jnp.abs(pos[:, None] - pos[None, :]) <= half_window
    keep_mask = near[None] & (pos[None, None, :] < lengths[:, None, None])
    logits = (
        jnp.einsum("tqhe,tkhe->thqk", queries_h, keys_h, preferred_element_type=jnp.float32)
        * scale_factor
    )
    logits = jnp.where(keep_mask[:, None], logits, jnp.float32(-1e30))
    top_val = jnp.max(logits, axis=-1, keepdims=True)
    expo = jnp.exp(logits - top_val)
    attn_weights = (expo / jnp.sum(expo, axis=-1, keepdims=True)).astype(jnp.bfloat16)
    context = jnp.einsum(
        "thqk,tkhe->tqhe", attn_weights, values_h, preferred_element_type=jnp.float32
    )
    context = jnp.where(
        (pos[None, :] < lengths[:, None])[:, :, None, None], context, jnp.float32(0.0)
    )
    return context.astype(jnp.bfloat16).reshape(
        queries_h.shape[0], seq_len, queries_h.shape[2] * HEAD_DIM
    )


def per_device(
    states,
    lengths,
    w_qkv,
    b_qkv,
    w_out,
    b_out,
    ln1_gain,
    ln1_shift,
    w_up,
    b_up,
    w_down,
    b_down,
    ln2_gain,
    ln2_shift,
    index_rows,
    cand_ids,
):
    tp_count = lax.axis_size("tp")
    tp_rank = lax.axis_index("tp")
    req_count = lax.axis_size("req")
    req_rank = lax.axis_index("req")
    text_count, row_share, model_width = states.shape
    quarter = cand_ids.shape[1]
    full_states = lax.all_gather(states, "tp", axis=1, tiled=True)
    device_count = req_count * tp_count
    gathered_ids = lax.all_to_all(
        jnp.broadcast_to(cand_ids[None], (device_count,) + cand_ids.shape),
        ("req", "tp"),
        0,
        0,
        tiled=True,
    )
    full_states, gathered_ids = lax.optimization_barrier((full_states, gathered_ids))
    seq_len = full_states.shape[1]
    local_width = w_qkv.shape[2]
    heads_here = local_width // HEAD_DIM
    projected = (
        jnp.einsum("tsd,dce->tsce", full_states, w_qkv, preferred_element_type=jnp.float32) + b_qkv
    ).astype(jnp.bfloat16)
    queries_h = projected[:, :, 0].reshape(text_count, seq_len, heads_here, HEAD_DIM)
    keys_h = projected[:, :, 1].reshape(text_count, seq_len, heads_here, HEAD_DIM)
    values_h = projected[:, :, 2].reshape(text_count, seq_len, heads_here, HEAD_DIM)
    context = window_attention(queries_h, keys_h, values_h, lengths)
    partial_value = jnp.einsum("tsk,kd->tsd", context, w_out, preferred_element_type=jnp.float32)
    attn_sum = lax.psum(partial_value.astype(jnp.bfloat16), "tp").astype(jnp.float32)
    normed_full = layer_norm(
        full_states.astype(jnp.float32) + attn_sum + b_out, ln1_gain, ln1_shift
    ).astype(jnp.bfloat16)
    normed_local = lax.dynamic_slice_in_dim(normed_full, tp_rank * row_share, row_share, 1)
    up_act = jax.nn.gelu(
        jnp.einsum("tsd,df->tsf", normed_full, w_up, preferred_element_type=jnp.float32) + b_up,
        approximate=False,
    ).astype(jnp.bfloat16)
    down_part = jnp.einsum("tsf,fd->tsd", up_act, w_down, preferred_element_type=jnp.float32)
    down_sum = lax.psum_scatter(
        down_part.astype(jnp.bfloat16), "tp", scatter_dimension=1, tiled=True
    ).astype(jnp.float32)
    hidden_out = layer_norm(
        normed_local.astype(jnp.float32) + down_sum + b_down, ln2_gain, ln2_shift
    ).astype(jnp.bfloat16)
    positions = tp_rank * row_share + jnp.arange(row_share, dtype=jnp.int32)
    is_valid = positions[None, :] < lengths[:, None]
    local_pool = jnp.sum(
        jnp.where(is_valid[:, :, None], hidden_out.astype(jnp.float32), jnp.float32(0.0)), axis=1
    )
    pooled = lax.psum(local_pool, "tp") / lengths.astype(jnp.float32)[:, None]
    query_vec = (
        pooled * lax.rsqrt(jnp.mean(pooled * pooled, axis=-1, keepdims=True) + norm_eps)
    ).astype(jnp.bfloat16)
    all_queries = lax.all_to_all(
        jnp.broadcast_to(query_vec[None], (req_count,) + query_vec.shape), "req", 0, 0, tiled=True
    ).reshape(req_count * text_count, model_width)
    all_ids = (
        gathered_ids.reshape(req_count, tp_count, text_count, quarter)
        .transpose(0, 2, 1, 3)
        .reshape(req_count * text_count, tp_count * quarter)
    )
    rows_here = index_rows.shape[0]
    first_row = (req_rank * tp_count + tp_rank) * rows_here
    local_ids = all_ids - first_row
    is_owned = (local_ids >= 0) & (local_ids < rows_here)
    safe_ids = jnp.clip(local_ids, 0, rows_here - 1)
    all_scores = jnp.einsum(
        "td,rd->tr", all_queries, index_rows, preferred_element_type=jnp.float32
    )
    score_rows = jnp.take(all_scores.T, safe_ids.reshape(-1), axis=0).reshape(
        safe_ids.shape[0], safe_ids.shape[1], safe_ids.shape[0]
    )
    picked = jnp.einsum("tct->tc", score_rows)
    owner_terms = jnp.where(is_owned, picked, jnp.float32(0.0))
    owner_terms = (
        owner_terms.reshape(req_count, text_count, tp_count, quarter)
        .transpose(0, 2, 1, 3)
        .reshape(device_count, text_count, quarter)
    )
    scores = jnp.sum(lax.all_to_all(owner_terms, ("req", "tp"), 0, 0, tiled=True), axis=0)
    return (hidden_out, scores)


def solution(mesh):
    placed = (
        P("req", "tp", None),
        P("req"),
        P(None, None, "tp"),
        P(None, "tp"),
        P("tp", None),
        P(),
        P(),
        P(),
        P(None, "tp"),
        P("tp"),
        P("tp", None),
        P(),
        P(),
        P(),
        P(("req", "tp"), None),
        P("req", "tp"),
    )
    return jax.shard_map(
        per_device,
        mesh=mesh,
        in_specs=placed,
        out_specs=(P("req", "tp", None), P("req", "tp")),
        check_vma=False,
    )
```

profile of v0, /device:TPU:1, one launch (start us, length us, event | category | flops | bytes accessed | tf_op | source)
XLA Modules:
  0.0 250.8 jit_solution(11163683712787077177)
XLA Ops:
  7.2 0.7 all-gather.2.cloned.1.call-update
  7.9 1.4 broadcast_in_dim.50
  9.3 11.5 %all-to-all-start = ((s32[128,2,16]{2,1,0:T(2,128)}), s32[128,2,16]{2,1,0:T(2,128)S(1)}, u32[]{:S(2)}, u32[]{:S(2)}) async-start(s32[128,2,16]{2,1,0:T(2,128)} %broadcast_in_dim.50), calls=%async_computation | async-start | bytes 262144 | tf_op jit(solution)/shard_map/all_to_all | solution.py:70
  21.0 0.7 iota_compare_fusion.1
  22.0 8.8 %all-to-all-done = s32[128,2,16]{2,1,0:T(2,128)S(1)} async-done(((s32[128,2,16]{2,1,0:T(2,128)}), s32[128,2,16]{2,1,0:T(2,128)S(1)}, u32[]{:S(2)}, u32[]{:S(2)}) %all-to-all-start) | async-done | bytes 16416 | tf_op jit(solution)/shard_map/all_to_all | solution.py:70
  30.8 12.9 %all-gather.2.cloned.1.call-done = bf16[2,512,1024]{2,1,0:T(8,128)(2,1)} async-done(((bf16[2,128,1024]{2,1,0:T(8,128)(2,1)}), bf16[2,512,1024]{2,1,0:T(8,128)(2,1)}) %all-gather.2.cloned.1.call-update) | async-done | bytes 2097168 | tf_op jit(solution)/shard_map/all_gather | solution.py:68
  43.7 3.9 %add_convert_fusion.1 = bf16[2,512,3,256]{1,3,2,0:T(8,128)(2,1)S(1)} fusion(f32[3,256]{1,0:T(4,128)} %param.19, bf16[1024,3,256]{2,0,1:T(8,128)(2,1)} %param.18, bf16[2,512,1024]{2,1,0:T(8,128)(2,1)} %all-gather.2.cloned.1.call-done), kind=kOutput, calls=%fused_computation.37 | convolution fusion | flops 1612185600 | bytes 5245952 | tf_op jit(solution)/shard_map/tsd,dce->tsce/dot_general | solution.py:82
  47.6 1.1 fusion.106
  48.8 7.7 %fusion.107 = (f32[2,4,512]{2,1,0:T(4,128)S(1)}, f32[2,4,512,512]{2,3,1,0:T(8,128)}) fusion(pred[2,512,512]{1,2,0:T(8,128)(4,1)S(1)} %broadcast_and_fusion, bf16[2,512,4,64]{1,3,2,0:T(8,128)(2,1)} %bitcast.61, bf16[2,512,4,64]{1,3,2,0:T(8,128)(2,1)} %bitcast.60), kind=kOutput, calls=%fused_computation.147 | convolution fusion | flops 276824576 | bytes 9977856 | tf_op jit(solution)/shard_map/sub | solution.py:31
  56.4 4.3 %fusion.64 = bf16[2,4,64,512]{3,2,1,0:T(8,128)(2,1)S(1)} fusion(bf16[2,512,4,64]{1,3,2,0:T(8,128)(2,1)S(1)} %bitcast.59, f32[2,4,512,512]{2,3,1,0:T(8,128)} %get-tuple-element.16, f32[2,4,512]{2,1,0:T(4,128)S(1)} %get-tuple-element.15, pred[2,512]{1,0:T(4,128)(4,1)S(1)} %iota_compare_fusion.1), kind=kOutput, calls=%fused_computation.79 | convolution fusion | flops 273154048 | bytes 9454592 | tf_op jit(solution)/shard_map/thqk,tkhe->tqhe/dot_general | solution.py:33
  60.8 2.1 convolution_convert_fusion
  63.1 58.6 %all-reduce.2.cloned.1.call-done = bf16[2,512,1024]{2,1,0:T(8,128)(2,1)} async-done(((bf16[2,512,1024]{2,1,0:T(8,128)(2,1)}), bf16[2,512,1024]{2,1,0:T(8,128)(2,1)}) %all-reduce.2.cloned.1.call-update) | async-done | bytes 2097168 | tf_op jit(solution)/shard_map/psum | solution.py:89
  121.7 3.1 %fusion.15 = f32[2,512]{1,0:T(2,128)S(1)} fusion(bf16[2,512,1024]{2,1,0:T(8,128)(2,1)} %all-reduce.2.cloned.1.call-done, bf16[2,512,1024]{2,1,0:T(8,128)(2,1)} %all-gather.2.cloned.1.call-done, f32[1024]{0:T(1024)S(1)} %copy-done.6), kind=kLoop, calls=%fused_computation.36 | loop fusion | flops 5241856 | bytes 4202496 | tf_op jit(solution)/shard_map/reduce_sum | solution.py:13
  124.8 0.3 copy-done.2
  125.2 1.1 multiply_reduce_fusion
  126.3 1.2 add_convert_fusion
  127.6 3.4 %fusion.66 = (u8[512,1024]{1,0:T(8,128)(4,1)S(1)}, u8[512,1024]{1,0:T(8,128)(4,1)S(1)}, f32[2,512,1024]{2,1,0:T(8,128)S(1)}) fusion(f32[1024]{0:T(1024)S(1)} %copy-done.13, bf16[2,512,1024]{2,1,0:T(8,128)(2,1)S(1)} %add_convert_fusion, bf16[1024,1024]{1,0:T(8,128)(2,1)S(1)} %copy-done), kind=kOutput, calls=%fused_computation.86 | convolution fusion | flops 2161115136 | bytes 9441280 | tf_op jit(solution)/shard_map/tsd,df->tsf/dot_general | solution.py:95
  131.0 12.5 %fusion.53 = bf16[2,512,1024]{2,1,0:T(8,128)(2,1)} fusion(bf16[1024,1024]{1,0:T(8,128)(2,1)S(1)} %copy-done.12, f32[2,512,1024]{2,1,0:T(8,128)S(1)} %get-tuple-element.17, f32[1024]{0:T(1024)S(1)} %copy-done.13, u8[512,1024]{1,0:T(8,128)(4,1)S(1)} %get-tuple-element.7, u8[512,1024]{1,0:T(8,128)(4,1)S(1)} %get-tuple-element.6), kind=kOutput, calls=%fused_computation.75 | convolution fusion | flops 2222981120 | bytes 9441280 | tf_op jit(solution)/shard_map/tsf,fd->tsd/dot_general | solution.py:98
  144.4 28.7 %reduce-scatter.2.cloned.1.call-done = bf16[2,128,1024]{2,1,0:T(8,128)(2,1)} async-done(((bf16[2,512,1024]{2,1,0:T(8,128)(2,1)}), bf16[2,128,1024]{2,1,0:T(8,128)(2,1)}) %reduce-scatter.2.cloned.1.call-update) | async-done | bytes 524304 | tf_op jit(solution)/shard_map/reduce_scatter | solution.py:99
  173.1 1.4 fusion.69
  174.6 1.5 multiply_reduce_fusion.1
  176.2 2.4 select_reduce_fusion.1
  178.6 6.7 %psum.15 = f32[2,1024]{1,0:T(2,128)S(1)} all-reduce(f32[2,1024]{1,0:T(2,128)S(1)} %get-tuple-element.10), channel_id=1, replica_groups=mesh['req'=32,'tp'=4] {'tp'}, use_global_device_ids=true, to_apply=%region_9.10 | all-reduce | flops 2048 | bytes 16384 | tf_op jit(solution)/shard_map/psum | solution.py:110
  185.5 0.7 broadcast_in_dim.63
  186.2 9.7 %all-to-all-start.1 = ((bf16[32,2,1024]{2,1,0:T(2,128)(2,1)}), bf16[32,2,1024]{2,1,0:T(2,128)(2,1)S(1)}, u32[]{:S(2)}, u32[]{:S(2)}) async-start(bf16[32,2,1024]{2,1,0:T(2,128)(2,1)} %broadcast_in_dim.63), calls=%async_computation.2 | async-start | bytes 262144 | tf_op jit(solution)/shard_map/all_to_all | solution.py:114
  195.9 7.7 %all-to-all-done.1 = bf16[32,2,1024]{2,1,0:T(2,128)(2,1)S(1)} async-done(((bf16[32,2,1024]{2,1,0:T(2,128)(2,1)}), bf16[32,2,1024]{2,1,0:T(2,128)(2,1)S(1)}, u32[]{:S(2)}, u32[]{:S(2)}) %all-to-all-start.1) | async-done | bytes 131104 | tf_op jit(solution)/shard_map/all_to_all | solution.py:114
  203.7 6.0 %convolution_bitcast_fusion = f32[4096,64]{0,1:T(8,128)S(1)} fusion(bf16[64,1024]{1,0:T(8,128)(2,1)S(1)} %reshape.217, bf16[4096,1024]{1,0:T(8,128)(2,1)} %param.30), kind=kOutput, calls=%fused_computation.7 | convolution fusion | flops 536870912 | bytes 9568256 | tf_op jit(solution)/shard_map/td,rd->tr/dot_general | solution.py:127
  209.7 2.0 copy.49
  211.7 15.7 %gather_fusion = f32[4096,64]{1,0:T(8,128)} fusion(f32[4096,64]{1,0:T(8,128)} %copy.49, s32[4096]{0:T(1024)S(1)} %broadcast_clamp_fusion), kind=kCustom, calls=%fused_computation | custom fusion | bytes 2113536 | tf_op jit(solution)/shard_map/jit(_take)/gather | solution.py:130
  227.3 1.9 select_reduce_fusion
  229.6 13.9 %all_to_all.15 = f32[128,2,16]{2,1,0:T(2,128)S(1)} all-to-all(f32[128,2,16]{2,1,0:T(2,128)S(1)} %copy.53), channel_id=1, replica_groups=mesh['req'=32,'tp'=4] {'req','tp'}, dimensions={0} | all-to-all | bytes 32768 | tf_op jit(solution)/shard_map/all_to_all | solution.py:140
  243.5 0.7 reduce_sum.89
  (62 shorter events, 2.4 us)
Async XLA Ops:
  7.2 120.3 %copy-start = (bf16[1024,1024]{1,0:T(8,128)(2,1)S(1)}, bf16[1024,1024]{1,0:T(8,128)(2,1)}, u32[]{:S(2)}) copy-start(bf16[1024,1024]{1,0:T(8,128)(2,1)} %param.24) | copy-start | bytes 6291460
  7.2 36.5 %all-gather.2.cloned.1.call-start = ((), (), s32[]{:S(2)}) async-start(), calls=%async_computation.4 | async-start | bytes 2621440 | tf_op jit(solution)/shard_map/all_gather | solution.py:68
  9.3 21.6 %all-to-all-start = ((s32[128,2,16]{2,1,0:T(2,128)}), s32[128,2,16]{2,1,0:T(2,128)S(1)}, u32[]{:S(2)}, u32[]{:S(2)}) async-start(s32[128,2,16]{2,1,0:T(2,128)} %broadcast_in_dim.50), calls=%async_computation | async-start | bytes 262144 | tf_op jit(solution)/shard_map/all_to_all | solution.py:70
  20.8 100.9 %all-reduce.2.cloned.1.call-start = ((), (), s32[]{:S(2)}) async-start(), calls=%async_computation.5 | async-start | bytes 4194304 | tf_op jit(solution)/shard_map/psum | solution.py:89
  56.4 4.3 %copy-start.4 = (bf16[256,1024]{1,0:T(8,128)(2,1)S(1)}, bf16[256,1024]{1,0:T(8,128)(2,1)}, u32[]{:S(2)}) copy-start(bf16[256,1024]{1,0:T(8,128)(2,1)} %param.20) | copy-start | bytes 1572868
  60.8 60.9 %copy-start.6 = (f32[1024]{0:T(1024)S(1)}, f32[1024]{0:T(1024)}, u32[]{:S(2)}) copy-start(f32[1024]{0:T(1024)} %param.21) | copy-start | bytes 12292
  62.9 63.4 %copy-start.9 = (f32[1024]{0:T(1024)S(1)}, f32[1024]{0:T(1024)}, u32[]{:S(2)}) copy-start(f32[1024]{0:T(1024)} %param.23) | copy-start | bytes 12292
  62.9 63.4 %copy-start.10 = (f32[1024]{0:T(1024)S(1)}, f32[1024]{0:T(1024)}, u32[]{:S(2)}) copy-start(f32[1024]{0:T(1024)} %param.22) | copy-start | bytes 12292
  62.9 110.3 %reduce-scatter.2.cloned.1.call-start = ((), (), s32[]{:S(2)}) async-start(), calls=%async_computation.6 | async-start | bytes 2621440 | tf_op jit(solution)/shard_map/reduce_scatter | solution.py:99
  121.7 3.1 %copy-start.1 = (bf16[2,512,1024]{2,1,0:T(8,128)(2,1)S(1)}, bf16[2,512,1024]{2,1,0:T(8,128)(2,1)}, u32[]{:S(2)}) copy-start(bf16[2,512,1024]{2,1,0:T(8,128)(2,1)} %all-gather.2.cloned.1.call-done) | copy-start | bytes 6291460
  121.7 3.5 %copy-start.2 = (bf16[2,512,1024]{2,1,0:T(8,128)(2,1)S(1)}, bf16[2,512,1024]{2,1,0:T(8,128)(2,1)}, u32[]{:S(2)}) copy-start(bf16[2,512,1024]{2,1,0:T(8,128)(2,1)} %all-reduce.2.cloned.1.call-done) | copy-start | bytes 6291460
  126.2 1.3 copy-start.13
  127.5 3.4 %copy-start.3 = (bf16[2,512,1024]{2,1,0:T(8,128)(2,1)}, bf16[2,512,1024]{2,1,0:T(8,128)(2,1)S(1)}, u32[]{:S(2)}) copy-start(bf16[2,512,1024]{2,1,0:T(8,128)(2,1)S(1)} %add_convert_fusion) | copy-start | bytes 6291460
  127.5 3.4 %copy-start.12 = (bf16[1024,1024]{1,0:T(8,128)(2,1)S(1)}, bf16[1024,1024]{1,0:T(8,128)(2,1)}, u32[]{:S(2)}) copy-start(bf16[1024,1024]{1,0:T(8,128)(2,1)} %param.26) | copy-start | bytes 6291460
  130.9 12.5 %copy-start.11 = (s32[2]{0:T(128)S(1)}, s32[2]{0:T(128)}, u32[]{:S(2)}) copy-start(s32[2]{0:T(128)} %param.17) | copy-start | bytes 28
  131.0 42.2 %copy-start.5 = (f32[1024]{0:T(1024)S(1)}, f32[1024]{0:T(1024)}, u32[]{:S(2)}) copy-start(f32[1024]{0:T(1024)} %param.27) | copy-start | bytes 12292
  143.4 32.7 %copy-start.7 = (f32[1024]{0:T(1024)S(1)}, f32[1024]{0:T(1024)}, u32[]{:S(2)}) copy-start(f32[1024]{0:T(1024)} %param.29) | copy-start | bytes 12292
  143.4 32.7 %copy-start.8 = (f32[1024]{0:T(1024)S(1)}, f32[1024]{0:T(1024)}, u32[]{:S(2)}) copy-start(f32[1024]{0:T(1024)} %param.28) | copy-start | bytes 12292
  186.2 17.4 %all-to-all-start.1 = ((bf16[32,2,1024]{2,1,0:T(2,128)(2,1)}), bf16[32,2,1024]{2,1,0:T(2,128)(2,1)S(1)}, u32[]{:S(2)}, u32[]{:S(2)}) async-start(bf16[32,2,1024]{2,1,0:T(2,128)(2,1)} %broadcast_in_dim.63), calls=%async_computation.2 | async-start | bytes 262144 | tf_op jit(solution)/shard_map/all_to_all | solution.py:114
Sparse Core Ops, SparseCore 0:
  9.7 34.0 all-gather.1
  63.0 58.6 all-reduce.1
  143.6 29.5 reduce-scatter.1
where the time goes:
time: 251 us
  waiting for transfers between devices  117 us (47%)
  matrix products  39.8 us (16%)
  local copies, waits for them, and re-layouts  22.2 us (9%)
  starting transfers between devices  21.5 us (9%)
  blocking collectives  20.5 us (8%)
  other arithmetic  15.3 us (6%)
  between operations  14.1 us (6%)
    psum x1, waiting for transfers between devices, per_device(): lax.psum(partial_value.astype(jnp.bfloat16), 'tp').astype(jnp.float32)  58.6 us
    reduce_scatter x1, waiting for transfers between devices, per_device(): lax.psum_scatter(down_part.astype(jnp.bfloat16), 'tp', scatter_dimension=...  28.7 us
    gather x1, local copies, waits for them, and re-layouts, per_device(): jnp.take(all_scores.T, safe_ids.reshape(-1), axis=0)  15.7 us
    all_to_all x1, blocking collectives, per_device(): lax.all_to_all(owner_terms, ('req', 'tp'), 0, 0, tiled=True)  13.9 us
    all_gather x1, waiting for transfers between devices, per_device(): full_states = lax.all_gather(states, 'tp', axis=1, tiled=True)  12.9 us
    dot_general x1, matrix products, per_device(): jnp.einsum('tsf,fd->tsd', up_act, w_down, preferred_element_type=jnp.floa...  12.5 us
    all_to_all x1, starting transfers between devices, per_device(): lax.all_to_all(jnp.broadcast_to(cand_ids[None], (device_count,) + cand_id...  11.5 us
    all_to_all x1, starting transfers between devices, per_device(): lax.all_to_all(jnp.broadcast_to(query_vec[None], (req_count,) + query_vec...  9.67 us
  transfers between devices with their start and end apart: 5, of which 5 were waited for; matrix products, arithmetic and copies ran while one was open for 1% of the time, Pallas kernels for 0%

commit v1 on v0

--- a/solution.py
+++ b/solution.py
@@ -86,7 +86,9 @@
     values_h = projected[:, :, 2].reshape(text_count, seq_len, heads_here, HEAD_DIM)
     context = window_attention(queries_h, keys_h, values_h, lengths)
     partial_value = jnp.einsum("tsk,kd->tsd", context, w_out, preferred_element_type=jnp.float32)
-    attn_sum = lax.psum(partial_value.astype(jnp.bfloat16), "tp").astype(jnp.float32)
+    attn_sum = jnp.sum(lax.all_gather(partial_value.astype(jnp.bfloat16), "tp"), axis=0).astype(
+        jnp.float32
+    )
     normed_full = layer_norm(
         full_states.astype(jnp.float32) + attn_sum + b_out, ln1_gain, ln1_shift
     ).astype(jnp.bfloat16)

time: 251 us -> 285 us (1.14)
  waiting for transfers between devices: 117 us -> 143 us
  other arithmetic: 15.3 us -> 22.9 us
    all_gather x0 -> x1, waiting for transfers between devices: none -> 83.1 us  [per_device(): lax.all_gather(partial_value.astype(jnp.bfloat16), 'tp')]
    psum x1 -> x0, waiting for transfers between devices: 58.6 us -> none  [per_device(): lax.psum(partial_value.astype(jnp.bfloat16), 'tp').astype(jnp.float32)]
    reduce_sum x0 -> x1, other arithmetic: none -> 7.42 us  [per_device(): jnp.sum(lax.all_gather(partial_value.astype(jnp.bfloat16), 'tp'), axis=0)]
where the time goes in v1:
time: 285 us; the launch traced here: 284 us
  waiting for transfers between devices  143 us (50%)
  matrix products  39.8 us (14%)
  other arithmetic  22.9 us (8%)
  local copies, waits for them, and re-layouts  22.2 us (8%)
  starting transfers between devices  21.5 us (8%)
  blocking collectives  20.5 us (7%)
  between operations  14.1 us (5%)
    all_gather x1, waiting for transfers between devices, per_device(): lax.all_gather(partial_value.astype(jnp.bfloat16), 'tp')  83.1 us
    reduce_scatter x1, waiting for transfers between devices, per_device(): lax.psum_scatter(down_part.astype(jnp.bfloat16), 'tp', scatter_dimension=...  29.9 us
    gather x1, local copies, waits for them, and re-layouts, per_device(): jnp.take(all_scores.T, safe_ids.reshape(-1), axis=0)  15.7 us
    all_to_all x1, blocking collectives, per_device(): lax.all_to_all(owner_terms, ('req', 'tp'), 0, 0, tiled=True)  13.9 us
    all_gather x1, waiting for transfers between devices, per_device(): full_states = lax.all_gather(states, 'tp', axis=1, tiled=True)  12.9 us
    dot_general x1, matrix products, per_device(): jnp.einsum('tsf,fd->tsd', up_act, w_down, preferred_element_type=jnp.floa...  12.5 us
    all_to_all x1, starting transfers between devices, per_device(): lax.all_to_all(jnp.broadcast_to(cand_ids[None], (device_count,) + cand_id...  11.5 us
    all_to_all x1, starting transfers between devices, per_device(): lax.all_to_all(jnp.broadcast_to(query_vec[None], (req_count,) + query_vec...  9.7 us
  transfers between devices with their start and end apart: 5, of which 5 were waited for; matrix products, arithmetic and copies ran while one was open for 1% of the time, Pallas kernels for 0%

profile of v1, /device:TPU:1, one launch (start us, length us, event | category | flops | bytes accessed | tf_op | source)
XLA Modules:
  0.0 284.0 jit_solution(13206694985377034282)
XLA Ops:
  7.2 0.7 all-gather.4.cloned.1.call-update
  7.9 1.4 broadcast_in_dim.50
  9.3 11.5 %all-to-all-start = ((s32[128,2,16]{2,1,0:T(2,128)}), s32[128,2,16]{2,1,0:T(2,128)S(1)}, u32[]{:S(2)}, u32[]{:S(2)}) async-start(s32[128,2,16]{2,1,0:T(2,128)} %broadcast_in_dim.50), calls=%async_computation | async-start | bytes 262144 | tf_op jit(solution)/shard_map/all_to_all | solution.py:70
  21.0 0.7 iota_compare_fusion.1
  22.1 8.8 %all-to-all-done = s32[128,2,16]{2,1,0:T(2,128)S(1)} async-done(((s32[128,2,16]{2,1,0:T(2,128)}), s32[128,2,16]{2,1,0:T(2,128)S(1)}, u32[]{:S(2)}, u32[]{:S(2)}) %all-to-all-start) | async-done | bytes 16416 | tf_op jit(solution)/shard_map/all_to_all | solution.py:70
  30.8 12.9 %all-gather.4.cloned.1.call-done = bf16[2,512,1024]{2,1,0:T(8,128)(2,1)} async-done(((bf16[2,128,1024]{2,1,0:T(8,128)(2,1)}), bf16[2,512,1024]{2,1,0:T(8,128)(2,1)}) %all-gather.4.cloned.1.call-update) | async-done | bytes 2097168 | tf_op jit(solution)/shard_map/all_gather | solution.py:68
  43.7 3.9 %add_convert_fusion.1 = bf16[2,512,3,256]{1,3,2,0:T(8,128)(2,1)S(1)} fusion(f32[3,256]{1,0:T(4,128)} %param.19, bf16[1024,3,256]{2,0,1:T(8,128)(2,1)} %param.18, bf16[2,512,1024]{2,1,0:T(8,128)(2,1)} %all-gather.4.cloned.1.call-done), kind=kOutput, calls=%fused_computation.37 | convolution fusion | flops 1612185600 | bytes 5245952 | tf_op jit(solution)/shard_map/tsd,dce->tsce/dot_general | solution.py:82
  47.6 1.1 fusion.106
  48.8 7.7 %fusion.107 = (f32[2,4,512]{2,1,0:T(4,128)S(1)}, f32[2,4,512,512]{2,3,1,0:T(8,128)}) fusion(pred[2,512,512]{1,2,0:T(8,128)(4,1)S(1)} %broadcast_and_fusion, bf16[2,512,4,64]{1,3,2,0:T(8,128)(2,1)} %bitcast.63, bf16[2,512,4,64]{1,3,2,0:T(8,128)(2,1)} %bitcast.62), kind=kOutput, calls=%fused_computation.147 | convolution fusion | flops 276824576 | bytes 9977856 | tf_op jit(solution)/shard_map/sub | solution.py:31
  56.4 4.3 %fusion.64 = bf16[2,4,64,512]{3,2,1,0:T(8,128)(2,1)S(1)} fusion(bf16[2,512,4,64]{1,3,2,0:T(8,128)(2,1)S(1)} %bitcast.61, f32[2,4,512,512]{2,3,1,0:T(8,128)} %get-tuple-element.16, f32[2,4,512]{2,1,0:T(4,128)S(1)} %get-tuple-element.15, pred[2,512]{1,0:T(4,128)(4,1)S(1)} %iota_compare_fusion.1), kind=kOutput, calls=%fused_computation.79 | convolution fusion | flops 273154048 | bytes 9454592 | tf_op jit(solution)/shard_map/thqk,tkhe->tqhe/dot_general | solution.py:33
  60.8 2.1 convolution_convert_fusion
  63.1 83.1 %all-gather.6.cloned.1.call-done = bf16[8,512,1024]{2,1,0:T(8,128)(2,1)} async-done(((bf16[2,512,1024]{2,1,0:T(8,128)(2,1)}), bf16[8,512,1024]{2,1,0:T(8,128)(2,1)}) %all-gather.6.cloned.1.call-update) | async-done | bytes 8388624 | tf_op jit(solution)/shard_map/all_gather | solution.py:89
  146.1 7.4 %reduce_sum.94 = bf16[2,512,1024]{2,1,0:T(8,128)(2,1)} reduce(bf16[4,2,512,1024]{3,2,1,0:T(8,128)(2,1)} %bitcast.56, bf16[]{:T(256)} %constant.53.clone.1), dimensions={0}, to_apply=%region_2.3 | reduce | flops 3145728 | bytes 10485762 | tf_op jit(solution)/shard_map/reduce_sum | solution.py:89
  153.6 3.1 %fusion.15 = f32[2,512]{1,0:T(2,128)S(1)} fusion(bf16[2,512,1024]{2,1,0:T(8,128)(2,1)} %reduce_sum.94, bf16[2,512,1024]{2,1,0:T(8,128)(2,1)} %all-gather.4.cloned.1.call-done, f32[1024]{0:T(1024)S(1)} %copy-done.6), kind=kLoop, calls=%fused_computation.36 | loop fusion | flops 5241856 | bytes 4202496 | tf_op jit(solution)/shard_map/reduce_sum | solution.py:13
  157.0 1.1 multiply_reduce_fusion
  158.1 1.5 add_convert_fusion
  159.7 3.4 %fusion.66 = (u8[512,1024]{1,0:T(8,128)(4,1)S(1)}, u8[512,1024]{1,0:T(8,128)(4,1)S(1)}, f32[2,512,1024]{2,1,0:T(8,128)S(1)}) fusion(f32[1024]{0:T(1024)S(1)} %copy-done.13, bf16[2,512,1024]{2,1,0:T(8,128)(2,1)S(1)} %add_convert_fusion, bf16[1024,1024]{1,0:T(8,128)(2,1)S(1)} %copy-done), kind=kOutput, calls=%fused_computation.86 | convolution fusion | flops 2161115136 | bytes 9441280 | tf_op jit(solution)/shard_map/tsd,df->tsf/dot_general | solution.py:97
  163.1 12.5 %fusion.53 = bf16[2,512,1024]{2,1,0:T(8,128)(2,1)} fusion(bf16[1024,1024]{1,0:T(8,128)(2,1)S(1)} %copy-done.12, f32[2,512,1024]{2,1,0:T(8,128)S(1)} %get-tuple-element.17, f32[1024]{0:T(1024)S(1)} %copy-done.13, u8[512,1024]{1,0:T(8,128)(4,1)S(1)} %get-tuple-element.7, u8[512,1024]{1,0:T(8,128)(4,1)S(1)} %get-tuple-element.6), kind=kOutput, calls=%fused_computation.75 | convolution fusion | flops 2222981120 | bytes 9441280 | tf_op jit(solution)/shard_map/tsf,fd->tsd/dot_general | solution.py:100
  176.5 29.9 %reduce-scatter.2.cloned.1.call-done = bf16[2,128,1024]{2,1,0:T(8,128)(2,1)} async-done(((bf16[2,512,1024]{2,1,0:T(8,128)(2,1)}), bf16[2,128,1024]{2,1,0:T(8,128)(2,1)}) %reduce-scatter.2.cloned.1.call-update) | async-done | bytes 524304 | tf_op jit(solution)/shard_map/reduce_scatter | solution.py:101
  206.4 1.4 fusion.69
  207.9 1.5 multiply_reduce_fusion.1
  209.4 2.4 select_reduce_fusion.1
  211.8 6.6 %psum.7 = f32[2,1024]{1,0:T(2,128)S(1)} all-reduce(f32[2,1024]{1,0:T(2,128)S(1)} %get-tuple-element.10), channel_id=1, replica_groups=mesh['req'=32,'tp'=4] {'tp'}, use_global_device_ids=true, to_apply=%region_9.10 | all-reduce | flops 2048 | bytes 16384 | tf_op jit(solution)/shard_map/psum | solution.py:112
  218.8 0.7 broadcast_in_dim.63
  219.5 9.7 %all-to-all-start.1 = ((bf16[32,2,1024]{2,1,0:T(2,128)(2,1)}), bf16[32,2,1024]{2,1,0:T(2,128)(2,1)S(1)}, u32[]{:S(2)}, u32[]{:S(2)}) async-start(bf16[32,2,1024]{2,1,0:T(2,128)(2,1)} %broadcast_in_dim.63), calls=%async_computation.2 | async-start | bytes 262144 | tf_op jit(solution)/shard_map/all_to_all | solution.py:116
  229.2 7.7 %all-to-all-done.1 = bf16[32,2,1024]{2,1,0:T(2,128)(2,1)S(1)} async-done(((bf16[32,2,1024]{2,1,0:T(2,128)(2,1)}), bf16[32,2,1024]{2,1,0:T(2,128)(2,1)S(1)}, u32[]{:S(2)}, u32[]{:S(2)}) %all-to-all-start.1) | async-done | bytes 131104 | tf_op jit(solution)/shard_map/all_to_all | solution.py:116
  236.9 6.0 %convolution_bitcast_fusion = f32[4096,64]{0,1:T(8,128)S(1)} fusion(bf16[64,1024]{1,0:T(8,128)(2,1)S(1)} %reshape.217, bf16[4096,1024]{1,0:T(8,128)(2,1)} %param.30), kind=kOutput, calls=%fused_computation.7 | convolution fusion | flops 536870912 | bytes 9568256 | tf_op jit(solution)/shard_map/td,rd->tr/dot_general | solution.py:129
  243.0 2.0 copy.49
  244.9 15.7 %gather_fusion = f32[4096,64]{1,0:T(8,128)} fusion(f32[4096,64]{1,0:T(8,128)} %copy.49, s32[4096]{0:T(1024)S(1)} %broadcast_clamp_fusion), kind=kCustom, calls=%fused_computation | custom fusion | bytes 2113536 | tf_op jit(solution)/shard_map/jit(_take)/gather | solution.py:132
  260.6 1.9 select_reduce_fusion
  262.9 13.9 %all_to_all.15 = f32[128,2,16]{2,1,0:T(2,128)S(1)} all-to-all(f32[128,2,16]{2,1,0:T(2,128)S(1)} %copy.53), channel_id=1, replica_groups=mesh['req'=32,'tp'=4] {'req','tp'}, dimensions={0} | all-to-all | bytes 32768 | tf_op jit(solution)/shard_map/all_to_all | solution.py:142
  276.8 0.7 reduce_sum.102
  (63 shorter events, 2.8 us)
Async XLA Ops:
  7.2 152.4 %copy-start = (bf16[1024,1024]{1,0:T(8,128)(2,1)S(1)}, bf16[1024,1024]{1,0:T(8,128)(2,1)}, u32[]{:S(2)}) copy-start(bf16[1024,1024]{1,0:T(8,128)(2,1)} %param.24) | copy-start | bytes 6291460
  7.2 36.5 %all-gather.4.cloned.1.call-start = ((), (), s32[]{:S(2)}) async-start(), calls=%async_computation.4 | async-start | bytes 2621440 | tf_op jit(solution)/shard_map/all_gather | solution.py:68
  9.3 21.6 %all-to-all-start = ((s32[128,2,16]{2,1,0:T(2,128)}), s32[128,2,16]{2,1,0:T(2,128)S(1)}, u32[]{:S(2)}, u32[]{:S(2)}) async-start(s32[128,2,16]{2,1,0:T(2,128)} %broadcast_in_dim.50), calls=%async_computation | async-start | bytes 262144 | tf_op jit(solution)/shard_map/all_to_all | solution.py:70
  20.8 125.3 %all-gather.6.cloned.1.call-start = ((), (), s32[]{:S(2)}) async-start(), calls=%async_computation.6 | async-start | bytes 10485760 | tf_op jit(solution)/shard_map/all_gather | solution.py:89
  56.4 4.3 %copy-start.4 = (bf16[256,1024]{1,0:T(8,128)(2,1)S(1)}, bf16[256,1024]{1,0:T(8,128)(2,1)}, u32[]{:S(2)}) copy-start(bf16[256,1024]{1,0:T(8,128)(2,1)} %param.20) | copy-start | bytes 1572868
  62.8 143.6 %reduce-scatter.2.cloned.1.call-start = ((), (), s32[]{:S(2)}) async-start(), calls=%async_computation.5 | async-start | bytes 2621440 | tf_op jit(solution)/shard_map/reduce_scatter | solution.py:101
  146.1 7.4 %copy-start.6 = (f32[1024]{0:T(1024)S(1)}, f32[1024]{0:T(1024)}, u32[]{:S(2)}) copy-start(f32[1024]{0:T(1024)} %param.21) | copy-start | bytes 12292
  153.6 3.2 %copy-start.1 = (bf16[2,512,1024]{2,1,0:T(8,128)(2,1)S(1)}, bf16[2,512,1024]{2,1,0:T(8,128)(2,1)}, u32[]{:S(2)}) copy-start(bf16[2,512,1024]{2,1,0:T(8,128)(2,1)} %reduce_sum.94) | copy-start | bytes 6291460
  153.6 3.5 %copy-start.2 = (bf16[2,512,1024]{2,1,0:T(8,128)(2,1)S(1)}, bf16[2,512,1024]{2,1,0:T(8,128)(2,1)}, u32[]{:S(2)}) copy-start(bf16[2,512,1024]{2,1,0:T(8,128)(2,1)} %all-gather.4.cloned.1.call-done) | copy-start | bytes 6291460
  153.6 4.6 %copy-start.9 = (f32[1024]{0:T(1024)S(1)}, f32[1024]{0:T(1024)}, u32[]{:S(2)}) copy-start(f32[1024]{0:T(1024)} %param.23) | copy-start | bytes 12292
  153.6 4.6 %copy-start.10 = (f32[1024]{0:T(1024)S(1)}, f32[1024]{0:T(1024)}, u32[]{:S(2)}) copy-start(f32[1024]{0:T(1024)} %param.22) | copy-start | bytes 12292
  158.1 1.5 copy-start.13
  159.6 3.4 %copy-start.3 = (bf16[2,512,1024]{2,1,0:T(8,128)(2,1)}, bf16[2,512,1024]{2,1,0:T(8,128)(2,1)S(1)}, u32[]{:S(2)}) copy-start(bf16[2,512,1024]{2,1,0:T(8,128)(2,1)S(1)} %add_convert_fusion) | copy-start | bytes 6291460
  159.6 3.4 %copy-start.12 = (bf16[1024,1024]{1,0:T(8,128)(2,1)S(1)}, bf16[1024,1024]{1,0:T(8,128)(2,1)}, u32[]{:S(2)}) copy-start(bf16[1024,1024]{1,0:T(8,128)(2,1)} %param.26) | copy-start | bytes 6291460
  163.0 12.5 %copy-start.11 = (s32[2]{0:T(128)S(1)}, s32[2]{0:T(128)}, u32[]{:S(2)}) copy-start(s32[2]{0:T(128)} %param.17) | copy-start | bytes 28
  163.1 43.4 %copy-start.5 = (f32[1024]{0:T(1024)S(1)}, f32[1024]{0:T(1024)}, u32[]{:S(2)}) copy-start(f32[1024]{0:T(1024)} %param.27) | copy-start | bytes 12292
  175.5 33.9 %copy-start.7 = (f32[1024]{0:T(1024)S(1)}, f32[1024]{0:T(1024)}, u32[]{:S(2)}) copy-start(f32[1024]{0:T(1024)} %param.29) | copy-start | bytes 12292
  175.5 33.9 %copy-start.8 = (f32[1024]{0:T(1024)S(1)}, f32[1024]{0:T(1024)}, u32[]{:S(2)}) copy-start(f32[1024]{0:T(1024)} %param.28) | copy-start | bytes 12292
  219.5 17.4 %all-to-all-start.1 = ((bf16[32,2,1024]{2,1,0:T(2,128)(2,1)}), bf16[32,2,1024]{2,1,0:T(2,128)(2,1)S(1)}, u32[]{:S(2)}, u32[]{:S(2)}) async-start(bf16[32,2,1024]{2,1,0:T(2,128)(2,1)} %broadcast_in_dim.63), calls=%async_computation.2 | async-start | bytes 262144 | tf_op jit(solution)/shard_map/all_to_all | solution.py:116
Sparse Core Ops, SparseCore 0:
  9.7 34.0 all-gather.3
  63.0 83.1 all-gather.5
  175.7 30.6 reduce-scatter.1
